TPU v7x, 32 devices: a whole 2x2x4 slice. The times are simulated.
32 devices in a mesh: rows: 4 (over y, x), cols: 8 (over z, core).
Axes of the slice: x: 2, y: 2, z: 4, core: 2. Of those that a mesh axis runs over, the one named last changes fastest.
Arguments:
- counts: bfloat16 [2048, 65536], P('rows', 'cols'), may hold values from 0 to 12, as said below
- start_a: float32 [2048, 128], P(('rows', 'cols')), may hold values from -0.4 to 0.4
- start_b: float32 [4096, 128], P(('cols', 'rows')), may hold values from -0.4 to 0.4
- start_c: float32 [16, 128], replicated, may hold values from -0.4 to 0.4
Outputs:
- factor_a: float32 [2048, 128], P(('rows', 'cols'))
- factor_b: float32 [4096, 128], P(('cols', 'rows'))
- factor_c: float32 [16, 128], replicated
Inputs may be any that keep to these rules, and one draw needn't show every extreme that they name: counts holds whole numbers.
All inputs are finite; a program needn't handle non-finite values.
Results may differ from a plain program's by a relative error of at most 0.009.
Values may be sent and summed in bfloat16 or wider, within the bound.
A program may use at most 128 MiB of HBM per device.

v0:
```python
import math

import jax
import jax.numpy as jnp
from jax import lax
from jax.sharding import PartitionSpec as P

ITERS = 2


def local(counts, start_a, start_b, start_c):
    rows_here, flat_width = counts.shape
    depth = start_c.shape[0]
    cols_here = flat_width // depth
    total_i = rows_here * lax.axis_size("rows")
    total_j = cols_here * lax.axis_size("cols")
    rate_a = 0.3 / math.sqrt(total_j * depth)
    rate_b = 0.3 / math.sqrt(total_i * depth)
    rate_c = 0.3 / math.sqrt(total_i * total_j)
    local_a, local_b, shared_c = (start_a, start_b, start_c)
    for iteration in range(ITERS):
        low_a = lax.all_gather(local_a.astype(jnp.bfloat16), "cols", axis=0, tiled=True)
        low_b = lax.all_gather(local_b.astype(jnp.bfloat16), "rows", axis=0, tiled=True)
        low_b_wide = low_b.astype(jnp.float32)
        scaled = (low_b_wide[:, None, :] * shared_c[None, :, :]).astype(jnp.bfloat16)
        scaled = scaled.reshape(cols_here * depth, shared_c.shape[1])
        log_rate = lax.dot_general(
            low_a, scaled, (((1,), (1,)), ((), ())), preferred_element_type=jnp.float32
        )
        residual = (jnp.exp(log_rate) - counts.astype(jnp.float32)).astype(jnp.bfloat16)
        grad_a = jnp.dot(residual, scaled, preferred_element_type=jnp.float32)
        mixed = lax.dot_general(
            residual, low_a, (((0,), (0,)), ((), ())), preferred_element_type=jnp.float32
        )
        mixed = mixed.reshape(cols_here, depth, shared_c.shape[1])
        grad_b = jnp.sum(mixed * shared_c[None, :, :], axis=1)
        grad_c = jnp.sum(mixed * low_b_wide[:, None, :], axis=0)
        summed_a = lax.psum_scatter(grad_a, "cols", scatter_dimension=0, tiled=True)
        summed_b = lax.psum_scatter(grad_b, "rows", scatter_dimension=0, tiled=True)
        local_a = local_a - rate_a * summed_a
        local_b = local_b - rate_b * summed_b
        partial_c = lax.psum(grad_c, "rows")
        summed_c = lax.psum(partial_c, "cols")
        shared_c = shared_c - rate_c * summed_c
    return (local_a, local_b, shared_c)


def solution(mesh):
    placed = (P("rows", "cols"), P(("rows", "cols"), None), P(("cols", "rows"), None), P())
    return jax.shard_map(
        local,
        mesh=mesh,
        in_specs=placed,
        out_specs=(P(("rows", "cols"), None), P(("cols", "rows"), None), P()),
        check_vma=False,
    )
```

profile of v0, /device:TPU:0, one launch (start us, length us, event | category | flops | bytes accessed | tf_op | source)
XLA Modules:
  0.0 196.8 jit_solution(8268836375010601139)
XLA Ops:
  7.2 0.0 copy-start.2
  7.2 0.0 copy-start.3
  7.2 0.0 copy-start.6
  7.2 0.0 reduce-scatter.5.cloned.1.call-start
  7.2 12.0 %copy.7 = bf16[512,8192]{0,1:T(8,128)(2,1)} copy(bf16[512,8192]{1,0:T(8,128)(2,1)} %param.4) | data formatting | bytes 16777216 | tf_op args[0]
  19.2 0.0 copy-done.2
  19.2 9.9 %all_gather.12 = bf16[512,128]{1,0:T(8,128)(2,1)S(1)} all-gather(bf16[128,128]{1,0:T(8,128)(2,1)S(1)} %convert_element_type.42), channel_id=1, replica_groups=mesh['rows'=4,'cols'=8] {'rows'}, dimensions={0}, use_global_device_ids=true | all-gather | bytes 163840 | tf_op jit(solution)/shard_map/all_gather | solution.py:23
  29.2 0.0 copy-done.3
  29.2 14.3 %all_gather.13 = bf16[512,128]{1,0:T(8,128)(2,1)S(1)} all-gather(bf16[64,128]{1,0:T(8,128)(2,1)S(1)} %convert_element_type.46), channel_id=1, replica_groups=mesh['rows'=4,'cols'=8] {'cols'}, dimensions={0}, use_global_device_ids=true | all-gather | bytes 147456 | tf_op jit(solution)/shard_map/all_gather | solution.py:22
  43.5 0.0 copy-done.6
  43.5 0.4 multiply_convert_fusion.1
  43.8 5.0 %fusion = bf16[512,8192]{0,1:T(8,128)(2,1)S(1)} fusion(bf16[512,8192]{0,1:T(8,128)(2,1)} %copy.7, bf16[8192,128]{1,0:T(8,128)(2,1)S(1)} %bitcast.22, bf16[512,128]{1,0:T(8,128)(2,1)S(1)} %all_gather.13), kind=kOutput, calls=%fused_computation.2 | convolution fusion | flops 1086324736 | bytes 19005440 | tf_op jit(solution)/shard_map/dot_general | solution.py:27
  48.9 0.0 copy-start
  48.9 3.2 %copy-done = bf16[512,8192]{0,1:T(8,128)(2,1)} copy-done((bf16[512,8192]{0,1:T(8,128)(2,1)}, bf16[512,8192]{0,1:T(8,128)(2,1)S(1)}, u32[]{:S(2)}) %copy-start) | copy-done | bytes 8388632
  52.1 3.0 %fusion.4 = f32[512,128]{1,0:T(8,128)} fusion(bf16[512,8192]{0,1:T(8,128)(2,1)S(1)} %fusion, bf16[8192,128]{1,0:T(8,128)(2,1)S(1)} %bitcast.23), kind=kOutput, calls=%fused_computation.18 | convolution fusion | flops 1073741824 | bytes 10747904 | tf_op jit(solution)/shard_map/dot_general | solution.py:31
  55.1 0.0 reduce-scatter.5.cloned.1.call-update
  55.2 0.0 reduce-scatter.7.cloned.1.call-start
  55.2 8.4 %multiply_reduce_fusion.3 = (f32[512,128]{1,0:T(8,128)}, f32[8192,128]{1,0:T(8,128)}) fusion(f32[16,128]{1,0:T(8,128)S(1)} %copy-done.6, bf16[512,8192]{0,1:T(8,128)(2,1)} %copy-done, bf16[512,128]{1,0:T(8,128)(2,1)S(1)} %all_gather.13), kind=kOutput, calls=%fused_computation.8 | convolution fusion | flops 1075773440 | bytes 12984320 | tf_op jit(solution)/shard_map/dot_general | solution.py:32
  63.6 0.0 reduce-scatter.7.cloned.1.call-update
  63.6 0.0 reduce-scatter.9.cloned.1.call-start
  63.6 2.8 %multiply_reduce_fusion.2 = f32[16,128]{1,0:T(8,128)S(1)} fusion(f32[512,16,128]{2,1,0:T(8,128)} %bitcast.20, f32[512,128]{1,0:T(8,128)S(1)} %convert_element_type.43), kind=kLoop, calls=%fused_computation.7 | loop fusion | flops 2095104 | bytes 4464640 | tf_op jit(solution)/shard_map/reduce_sum | solution.py:37
  66.4 9.1 %psum.28 = f32[16,128]{1,0:T(8,128)S(1)} all-reduce(f32[16,128]{1,0:T(8,128)S(1)} %multiply_reduce_fusion.2), channel_id=1, replica_groups=mesh['rows'=4,'cols'=8] {'rows'}, use_global_device_ids=true, to_apply=%region_4.0 | all-reduce | flops 2048 | bytes 16384 | tf_op jit(solution)/shard_map/psum | solution.py:42
  75.5 15.1 %psum.29 = f32[16,128]{1,0:T(8,128)S(1)} all-reduce(f32[16,128]{1,0:T(8,128)S(1)} %psum.28), channel_id=1, replica_groups=mesh['rows'=4,'cols'=8] {'cols'}, use_global_device_ids=true, to_apply=%region_5.0 | all-reduce | flops 2048 | bytes 16384 | tf_op jit(solution)/shard_map/psum | solution.py:43
  90.7 0.0 reduce-scatter.5.cloned.1.call-done
  90.7 0.8 fusion.3
  91.5 13.9 %all_gather.14 = bf16[512,128]{1,0:T(8,128)(2,1)S(1)} all-gather(bf16[64,128]{1,0:T(8,128)(2,1)S(1)} %fusion.3), channel_id=1, replica_groups=mesh['rows'=4,'cols'=8] {'cols'}, dimensions={0}, use_global_device_ids=true | all-gather | bytes 147456 | tf_op jit(solution)/shard_map/all_gather | solution.py:22
  105.4 6.0 %reduce-scatter.7.cloned.1.call-done = f32[128,128]{1,0:T(8,128)} async-done(((f32[512,128]{1,0:T(8,128)}), f32[128,128]{1,0:T(8,128)}) %reduce-scatter.7.cloned.1.call-update) | async-done | bytes 65552 | tf_op jit(solution)/shard_map/reduce_scatter | solution.py:39
  111.4 0.8 fusion.2
  112.3 8.7 %all_gather.15 = bf16[512,128]{1,0:T(8,128)(2,1)S(1)} all-gather(bf16[128,128]{1,0:T(8,128)(2,1)S(1)} %fusion.2), channel_id=1, replica_groups=mesh['rows'=4,'cols'=8] {'rows'}, dimensions={0}, use_global_device_ids=true | all-gather | bytes 163840 | tf_op jit(solution)/shard_map/all_gather | solution.py:23
  121.0 0.4 multiply_convert_fusion
  121.3 5.0 %fusion.1 = bf16[512,8192]{0,1:T(8,128)(2,1)S(1)} fusion(bf16[512,8192]{0,1:T(8,128)(2,1)} %copy.7, bf16[512,128]{1,0:T(8,128)(2,1)S(1)} %all_gather.14, bf16[8192,128]{1,0:T(8,128)(2,1)S(1)} %bitcast.24), kind=kOutput, calls=%fused_computation.3 | convolution fusion | flops 1086324736 | bytes 19005440 | tf_op jit(solution)/shard_map/dot_general | solution.py:27
  126.4 0.0 copy-start.1
  126.4 3.2 %copy-done.1 = bf16[512,8192]{0,1:T(8,128)(2,1)} copy-done((bf16[512,8192]{0,1:T(8,128)(2,1)}, bf16[512,8192]{0,1:T(8,128)(2,1)S(1)}, u32[]{:S(2)}) %copy-start.1) | copy-done | bytes 8388632
  129.6 3.1 %fusion.5 = f32[512,128]{1,0:T(8,128)} fusion(bf16[512,8192]{0,1:T(8,128)(2,1)S(1)} %fusion.1, bf16[8192,128]{1,0:T(8,128)(2,1)S(1)} %bitcast.25), kind=kOutput, calls=%fused_computation.19 | convolution fusion | flops 1073741824 | bytes 10747904 | tf_op jit(solution)/shard_map/dot_general | solution.py:31
  132.7 0.0 reduce-scatter.9.cloned.1.call-update
  132.7 0.0 reduce-scatter.11.cloned.1.call-start
  132.7 8.4 %multiply_reduce_fusion.1 = (f32[512,128]{1,0:T(8,128)}, f32[8192,128]{1,0:T(8,128)}) fusion(f32[16,128]{1,0:T(8,128)S(1)} %multiply_subtract_fusion.5, bf16[512,8192]{0,1:T(8,128)(2,1)} %copy-done.1, bf16[512,128]{1,0:T(8,128)(2,1)S(1)} %all_gather.14), kind=kOutput, calls=%fused_computation.5 | convolution fusion | flops 1075773440 | bytes 12984320 | tf_op jit(solution)/shard_map/dot_general | solution.py:32
  141.2 0.0 copy-start.5
  141.2 0.0 reduce-scatter.11.cloned.1.call-update
  141.2 2.8 %multiply_reduce_fusion = f32[16,128]{1,0:T(8,128)S(1)} fusion(f32[512,16,128]{2,1,0:T(8,128)} %bitcast.21, f32[512,128]{1,0:T(8,128)S(1)} %convert_element_type.51), kind=kLoop, calls=%fused_computation.4 | loop fusion | flops 2095104 | bytes 4464640 | tf_op jit(solution)/shard_map/reduce_sum | solution.py:37
  144.0 9.1 %psum.30 = f32[16,128]{1,0:T(8,128)S(1)} all-reduce(f32[16,128]{1,0:T(8,128)S(1)} %multiply_reduce_fusion), channel_id=1, replica_groups=mesh['rows'=4,'cols'=8] {'rows'}, use_global_device_ids=true, to_apply=%region_10.0 | all-reduce | flops 2048 | bytes 16384 | tf_op jit(solution)/shard_map/psum | solution.py:42
  153.1 13.8 %psum.31 = f32[16,128]{1,0:T(8,128)S(1)} all-reduce(f32[16,128]{1,0:T(8,128)S(1)} %psum.30), channel_id=1, replica_groups=mesh['rows'=4,'cols'=8] {'cols'}, use_global_device_ids=true, to_apply=%region_11.0 | all-reduce | flops 2048 | bytes 16384 | tf_op jit(solution)/shard_map/psum | solution.py:43
  166.9 0.6 multiply_subtract_fusion.4
  167.5 0.0 copy-done.5
  167.5 1.4 multiply_subtract_fusion.2
  168.9 19.9 %reduce-scatter.11.cloned.1.call-done = f32[128,128]{1,0:T(8,128)} async-done(((f32[512,128]{1,0:T(8,128)}), f32[128,128]{1,0:T(8,128)}) %reduce-scatter.11.cloned.1.call-update) | async-done | bytes 65552 | tf_op jit(solution)/shard_map/reduce_scatter | solution.py:39
  188.8 0.0 copy-done.4
  188.8 1.5 multiply_subtract_fusion
  (7 shorter events, 0.1 us)
Async XLA Ops:
  7.2 12.0 %copy-start.2 = (f32[128,128]{1,0:T(8,128)S(1)}, f32[128,128]{1,0:T(8,128)}, u32[]{:S(2)}) copy-start(f32[128,128]{1,0:T(8,128)} %param.6) | copy-start | bytes 196612
  7.2 22.0 %copy-start.3 = (f32[64,128]{1,0:T(8,128)S(1)}, f32[64,128]{1,0:T(8,128)}, u32[]{:S(2)}) copy-start(f32[64,128]{1,0:T(8,128)} %param.5) | copy-start | bytes 98308
  7.2 36.3 %copy-start.6 = (f32[16,128]{1,0:T(8,128)S(1)}, f32[16,128]{1,0:T(8,128)}, u32[]{:S(2)}) copy-start(f32[16,128]{1,0:T(8,128)} %param.7) | copy-start | bytes 24580
  7.2 83.5 %reduce-scatter.5.cloned.1.call-start = ((), (), s32[]{:S(2)}) async-start(), calls=%async_computation.4 | async-start | bytes 294912 | tf_op jit(solution)/shard_map/reduce_scatter | solution.py:38
  48.9 3.2 %copy-start = (bf16[512,8192]{0,1:T(8,128)(2,1)}, bf16[512,8192]{0,1:T(8,128)(2,1)S(1)}, u32[]{:S(2)}) copy-start(bf16[512,8192]{0,1:T(8,128)(2,1)S(1)} %fusion) | copy-start | bytes 25165828
  55.2 56.3 %reduce-scatter.7.cloned.1.call-start = ((), (), s32[]{:S(2)}) async-start(), calls=%async_computation.5 | async-start | bytes 327680 | tf_op jit(solution)/shard_map/reduce_scatter | solution.py:39
  63.6 103.9 %reduce-scatter.9.cloned.1.call-start = ((), (), s32[]{:S(2)}) async-start(), calls=%async_computation.6 | async-start | bytes 294912 | tf_op jit(solution)/shard_map/reduce_scatter | solution.py:38
  126.4 3.2 %copy-start.1 = (bf16[512,8192]{0,1:T(8,128)(2,1)}, bf16[512,8192]{0,1:T(8,128)(2,1)S(1)}, u32[]{:S(2)}) copy-start(bf16[512,8192]{0,1:T(8,128)(2,1)S(1)} %fusion.1) | copy-start | bytes 25165828
  132.7 56.1 %reduce-scatter.11.cloned.1.call-start = ((), (), s32[]{:S(2)}) async-start(), calls=%async_computation.7 | async-start | bytes 327680 | tf_op jit(solution)/shard_map/reduce_scatter | solution.py:39
  141.2 26.4 %copy-start.5 = (f32[64,128]{1,0:T(8,128)S(1)}, f32[64,128]{1,0:T(8,128)}, u32[]{:S(2)}) copy-start(f32[64,128]{1,0:T(8,128)} %reduce-scatter.5.cloned.1.call-done) | copy-start | bytes 98308
  141.2 47.6 %copy-start.4 = (f32[128,128]{1,0:T(8,128)S(1)}, f32[128,128]{1,0:T(8,128)}, u32[]{:S(2)}) copy-start(f32[128,128]{1,0:T(8,128)} %reduce-scatter.7.cloned.1.call-done) | copy-start | bytes 196612
Sparse Core Ops, SparseCore 0:
  55.3 30.7 reduce-scatter.4
  88.9 22.4 reduce-scatter.6
  132.8 30.7 reduce-scatter.8
  166.2 22.4 reduce-scatter.10
where the time goes:
time: 198 us; the launch traced here: 197 us
  blocking collectives  94 us (47%)
  matrix products  33 us (17%)
  waiting for transfers between devices  26 us (13%)
  local copies, waits for them, and re-layouts  18.4 us (9%)
  between operations  13.9 us (7%)
  other arithmetic  11.4 us (6%)
    psum x2, blocking collectives, local(): summed_c = lax.psum(partial_c, 'cols')  29 us
    all_gather x2, blocking collectives, local(): lax.all_gather(local_a.astype(jnp.bfloat16), 'cols', axis=0, tiled=True)  28.2 us
    reduce_scatter x2, waiting for transfers between devices, local(): summed_b = lax.psum_scatter(grad_b, 'rows', scatter_dimension=0, tiled=True)  25.9 us
    all_gather x2, blocking collectives, local(): lax.all_gather(local_b.astype(jnp.bfloat16), 'rows', axis=0, tiled=True)  18.6 us
    unnamed x15, local copies, waits for them, and re-layouts  18.4 us
    psum x2, blocking collectives, local(): partial_c = lax.psum(grad_c, 'rows')  18.2 us
    dot_general x2, matrix products, local(): lax.dot_general(residual, low_a, (((0,), (0,)), ((), ())), preferred_elem...  16.8 us
    dot_general x2, matrix products, local(): lax.dot_general(low_a, scaled, (((1,), (1,)), ((), ())), preferred_elemen...  10.1 us
  transfers between devices with their start and end apart: 4, of which 2 were waited for; matrix products, arithmetic and copies ran while one was open for 13% of the time, Pallas kernels for 0%

commit v1 on v0

v1 whole, which is shorter than its diff:
```python
import functools
import math

import jax
import jax.numpy as jnp
from jax import lax
from jax.experimental import pallas as pl
from jax.experimental.pallas import tpu as pltpu
from jax.sharding import PartitionSpec as P

ITERS = 2
MESH = pl.DeviceIdType.MESH
F32 = jnp.float32
BF16 = jnp.bfloat16


def kernel(nr, nc, tile, rates, counts_hbm, a_in, b_in, c_in, a_out, b_out, c_out,
           counts, all_a, all_b, send_a, send_b, recv_a, recv_b, part_c, sum_c,
           trans_a, acc_a, acc_c, resid, scaled, grad_b,
           cnt_sem, ag_send, ag_recv, bg_send, bg_recv, ar_send, ar_recv, br_send, br_recv,
           c1_send, c1_recv, c2_send, c2_recv):
    row, col = lax.axis_index("rows"), lax.axis_index("cols")
    rate_a, rate_b, rate_c = rates
    own_a, rank = a_in.shape
    own_b = b_in.shape[0]
    depth = c_in.shape[0]
    tiles = counts.shape[0]
    per = tiles // nr
    width = tile // depth

    def peer(axis, me, n, off):
        p = lax.rem(me + off, n)
        return p, {axis: p}

    def load(t):
        return pltpu.make_async_copy(
            counts_hbm.at[:, pl.ds(pl.multiple_of(t * tile, tile), tile)], counts.at[t], cnt_sem.at[t])

    order = [lax.rem(row + 1 + d, nr) for d in range(nr)]
    for q in order:
        for s in range(per):
            load(q * per + s).start()

    all_a[0, col] = a_in[...].astype(BF16)
    all_b[0, row] = b_in[...].astype(BF16)

    barrier = pltpu.get_barrier_semaphore()
    for off in range(1, nc):
        pl.semaphore_signal(barrier, inc=1, device_id=peer("cols", col, nc, off)[1], device_id_type=MESH)
    for off in range(1, nr):
        pl.semaphore_signal(barrier, inc=1, device_id=peer("rows", row, nr, off)[1], device_id_type=MESH)
    pl.semaphore_wait(barrier, nc + nr - 2)

    def copy(src, dst, ss, rs, dev):
        return pltpu.make_async_remote_copy(
            src_ref=src, dst_ref=dst, send_sem=ss, recv_sem=rs, device_id=dev, device_id_type=MESH)

    class Spread:
        def __init__(self, buf, ss, rs, axis, me, n):
            self.args = (buf, ss, rs, axis, me, n)

        def out(self, off):
            buf, ss, rs, axis, me, n = self.args
            return copy(buf.at[me], buf.at[me], ss.at[off], rs.at[me], peer(axis, me, n, off)[1])

        def start(self):
            for off in range(1, self.args[5]):
                self.out(off).start()

        def wait_recv(self):
            buf, ss, rs, axis, me, n = self.args
            for off in range(1, n):
                p, dev = peer(axis, me, n, off)
                copy(buf.at[p], buf.at[p], ss.at[off], rs.at[p], dev).wait_recv()

        def wait_send(self):
            for off in range(1, self.args[5]):
                self.out(off).wait_send()

    class Scatter:
        def __init__(self, send, recv, ss, rs, axis, me, n):
            self.args = (send, recv, ss, rs, axis, me, n)

        def to(self, p):
            send, recv, ss, rs, axis, me, n = self.args
            return copy(send.at[p], recv.at[me], ss.at[p], rs.at[me], {axis: p})

        def peers(self):
            n = self.args[6]
            return [lax.rem(self.args[5] + off, n) for off in range(1, n)]

        def start(self):
            for p in self.peers():
                self.to(p).start()

        def wait_recv(self):
            send, recv, ss, rs, axis, me, n = self.args
            for p in self.peers():
                copy(send.at[p], recv.at[p], ss.at[p], rs.at[p], {axis: p}).wait_recv()

        def wait_send(self):
            for p in self.peers():
                self.to(p).wait_send()

    pending = []
    local_a, local_b, shared_c = a_in[...], b_in[...], c_in[...]
    gather_a = Spread(all_a.at[0], ag_send.at[0], ag_recv.at[0], "cols", col, nc)
    gather_b = Spread(all_b.at[0], bg_send.at[0], bg_recv.at[0], "rows", row, nr)
    gather_a.start()
    gather_b.start()
    pending += [gather_a, gather_b]

    for it in range(ITERS):
        gather_a.wait_recv()
        gather_b.wait_recv()
        rows_a = all_a[it].reshape(nc * own_a, rank)
        trans_a[...] = rows_a.T
        acc_a[...] = jnp.zeros_like(acc_a)
        acc_c[...] = jnp.zeros_like(acc_c)

        def produce(q, s, slot):
            t = q * per + s
            if it == 0:
                load(t).wait()
            rows_b = all_b[it, q, pl.ds(s * width, width), :].astype(F32)
            wide = (rows_b[:, None, :] * shared_c[None, :, :]).astype(BF16).reshape(tile, rank)
            scaled[slot] = wide
            log_rate = lax.dot_general(
                all_a[it].reshape(nc * own_a, rank), wide, (((1,), (1,)), ((), ())), preferred_element_type=F32)
            resid[slot] = (jnp.exp(log_rate) - counts[t].astype(F32)).astype(BF16)

        def consume(q, s, slot):
            acc_a[...] += jnp.dot(resid[slot], scaled[slot], preferred_element_type=F32)
            mixed = jnp.dot(trans_a[...], resid[slot], preferred_element_type=F32).T
            mixed = mixed.reshape(width, depth, rank)
            rows_b = all_b[it, q, pl.ds(s * width, width), :].astype(F32)
            grad_b[pl.ds(s * width, width), :] = jnp.sum(mixed * shared_c[None, :, :], axis=1)
            acc_c[...] += jnp.sum(mixed * rows_b[:, None, :], axis=0)

        scatter_b = Scatter(send_b.at[it], recv_b.at[it], br_send.at[it], br_recv.at[it], "rows", row, nr)
        produce(order[0], 0, 0)

        def step(d, carry):
            q = lax.rem(row + 1 + d, nr)
            for s in range(per):
                if s + 1 < per:
                    produce(q, s + 1, (s + 1) % 2)
                else:
                    @pl.when(d < nr - 1)
                    def _():
                        produce(lax.rem(q + 1, nr), 0, (s + 1) % 2)
                consume(q, s, s % 2)
            send_b[it, q] = grad_b[...].astype(BF16)

            @pl.when(d < nr - 1)
            def _():
                scatter_b.to(q).start()

            return carry

        lax.fori_loop(0, nr, step, 0)
        pending.append(scatter_b)

        for p in range(nc):
            send_a[it, p] = acc_a[pl.ds(p * own_a, own_a), :].astype(BF16)
        part_c[it, col] = acc_c[...].astype(BF16)
        scatter_a = Scatter(send_a.at[it], recv_a.at[it], ar_send.at[it], ar_recv.at[it], "cols", col, nc)
        scatter_a.start()
        cols_c = Spread(part_c.at[it], c1_send.at[it], c1_recv.at[it], "cols", col, nc)
        cols_c.start()
        pending += [scatter_a, cols_c]

        scatter_b.wait_recv()
        recv_b[it, row] = jnp.zeros((own_b, rank), BF16)
        total_b = grad_b[...] + jnp.sum(recv_b[it].astype(F32), axis=0)
        local_b = local_b - rate_b * total_b
        last = it == ITERS - 1
        if last:
            b_out[...] = local_b
        else:
            all_b[it + 1, row] = local_b.astype(BF16)
            gather_b = Spread(all_b.at[it + 1], bg_send.at[it + 1], bg_recv.at[it + 1], "rows", row, nr)
            gather_b.start()
            pending.append(gather_b)

        scatter_a.wait_recv()
        recv_a[it, col] = jnp.zeros((own_a, rank), BF16)
        own_rows = pl.ds(pl.multiple_of(col * own_a, own_a), own_a)
        total_a = acc_a[own_rows, :] + jnp.sum(recv_a[it].astype(F32), axis=0)
        local_a = local_a - rate_a * total_a
        if last:
            a_out[...] = local_a
        else:
            all_a[it + 1, col] = local_a.astype(BF16)
            gather_a = Spread(all_a.at[it + 1], ag_send.at[it + 1], ag_recv.at[it + 1], "cols", col, nc)
            gather_a.start()
            pending.append(gather_a)

        cols_c.wait_recv()
        sum_c[it, row] = jnp.sum(part_c[it].astype(F32), axis=0)
        rows_c = Spread(sum_c.at[it], c2_send.at[it], c2_recv.at[it], "rows", row, nr)
        rows_c.start()
        pending.append(rows_c)
        rows_c.wait_recv()
        shared_c = shared_c - rate_c * jnp.sum(sum_c[it], axis=0)
        if last:
            c_out[...] = shared_c

    for group in pending:
        group.wait_send()


def local(nr, nc, counts, start_a, start_b, start_c):
    rows_here, flat_width = counts.shape
    own_a, rank = start_a.shape
    own_b = start_b.shape[0]
    depth = start_c.shape[0]
    cols_here = flat_width // depth
    total_i, total_j = rows_here * nr, cols_here * nc
    rates = (0.3 / math.sqrt(total_j * depth), 0.3 / math.sqrt(total_i * depth), 0.3 / math.sqrt(total_i * total_j))
    tile = 512
    tiles = flat_width // tile
    vmem = pl.BlockSpec(memory_space=pltpu.VMEM)
    dma = pltpu.SemaphoreType.DMA
    return pl.pallas_call(
        functools.partial(kernel, nr, nc, tile, rates),
        out_shape=[jax.ShapeDtypeStruct(x.shape, F32) for x in (start_a, start_b, start_c)],
        in_specs=[pl.BlockSpec(memory_space=pl.ANY), vmem, vmem, vmem],
        out_specs=[vmem] * 3,
        scratch_shapes=[
            pltpu.VMEM((tiles, rows_here, tile), BF16),
            pltpu.VMEM((ITERS, nc, own_a, rank), BF16),
            pltpu.VMEM((ITERS, nr, own_b, rank), BF16),
            pltpu.VMEM((ITERS, nc, own_a, rank), BF16),
            pltpu.VMEM((ITERS, nr, own_b, rank), BF16),
            pltpu.VMEM((ITERS, nc, own_a, rank), BF16),
            pltpu.VMEM((ITERS, nr, own_b, rank), BF16),
            pltpu.VMEM((ITERS, nc, depth, rank), BF16),
            pltpu.VMEM((ITERS, nr, depth, rank), F32),
            pltpu.VMEM((rank, rows_here), BF16),
            pltpu.VMEM((rows_here, rank), F32),
            pltpu.VMEM((depth, rank), F32),
            pltpu.VMEM((2, rows_here, tile), BF16),
            pltpu.VMEM((2, tile, rank), BF16),
            pltpu.VMEM((own_b, rank), F32),
            dma((tiles,)),
            dma((ITERS, nc)), dma((ITERS, nc)), dma((ITERS, nr)), dma((ITERS, nr)),
            dma((ITERS, nc)), dma((ITERS, nc)), dma((ITERS, nr)), dma((ITERS, nr)),
            dma((ITERS, nc)), dma((ITERS, nc)), dma((ITERS, nr)), dma((ITERS, nr)),
        ],
        compiler_params=pltpu.CompilerParams(
            collective_id=0, has_side_effects=True, vmem_limit_bytes=56 * 1024 * 1024),
    )(counts, start_a, start_b, start_c)


def solution(mesh):
    nr, nc = mesh.shape["rows"], mesh.shape["cols"]
    placed = (P("rows", "cols"), P(("rows", "cols"), None), P(("cols", "rows"), None), P())
    return jax.shard_map(
        functools.partial(local, nr, nc),
        mesh=mesh,
        in_specs=placed,
        out_specs=(P(("rows", "cols"), None), P(("cols", "rows"), None), P()),
        check_vma=False,
    )
```

time: 198 us -> 55.6 us (0.28)
  blocking collectives: 94 us -> 0 us
  Pallas kernels: 0 us -> 50.5 us
  matrix products: 33 us -> 0 us
  waiting for transfers between devices: 26 us -> 0 us
  local copies, waits for them, and re-layouts: 18.4 us -> 4.14 us
  between operations: 13.9 us -> 0.64 us
  other arithmetic: 11.4 us -> 0 us
    pallas_call x0 -> x1, Pallas kernels: none -> 50.5 us  [local(): pl.pallas_call(functools.partial(kernel, nr, nc, tile, rates), out_shape=...]
    psum x4 -> x0, blocking collectives: 47.2 us -> none  [the longest x2 29 us: local(): summed_c = lax.psum(partial_c, 'cols')]
    all_gather x4 -> x0, blocking collectives: 46.8 us -> none  [the longest x2 28.2 us: local(): lax.all_gather(local_a.astype(jnp.bfloat16), 'cols', axis=0, tiled=True)]
    dot_general x6 -> x0, matrix products: 33 us -> none  [the longest x2 16.8 us: local(): lax.dot_general(residual, low_a, (((0,), (0,)), ((), ())), preferred_elem...]
    reduce_scatter x4 -> x0, waiting for transfers between devices: 25.9 us -> none  [the longest x2 25.9 us: local(): summed_b = lax.psum_scatter(grad_b, 'rows', scatter_dimension=0, tiled=True)]
    unnamed x15 -> x3, local copies, waits for them, and re-layouts: 18.4 us -> 4.14 us
    reduce_sum x2 -> x0, other arithmetic: 5.56 us -> none  [local(): grad_c = jnp.sum(mixed * low_b_wide[:, None, :], axis=0)]
    sub x4 -> x0, other arithmetic: 3.47 us -> none  [the longest x1 1.48 us: local(): local_b = local_b - rate_b * summed_b]
  transfers between devices with their start and end apart: 4 -> 0, of which waited for: 2 -> 0; matrix products, arithmetic and copies ran while one was open for 13% -> 0% of each run, Pallas kernels for 0% -> 0%
where the time goes in v1:
time: 55.6 us; the launch traced here: 55.3 us
  Pallas kernels  50.5 us (91%)
  local copies, waits for them, and re-layouts  4.14 us (7%)
  between operations  0.64 us (1%)
    pallas_call x1, Pallas kernels, local(): pl.pallas_call(functools.partial(kernel, nr, nc, tile, rates), out_shape=...  50.5 us
    unnamed x3, local copies, waits for them, and re-layouts  4.14 us

profile of v1, /device:TPU:0, one launch (start us, length us, event | category | flops | bytes accessed | tf_op | source)
XLA Modules:
  0.0 55.3 jit_solution(2440914384359519019)
XLA Ops:
  0.6 50.5 %shard_map.67 = (f32[64,128]{1,0:T(8,128)}, f32[128,128]{1,0:T(8,128)}, f32[16,128]{1,0:T(8,128)}) custom-call(bf16[512,8192]{1,0:T(8,128)(2,1)} %counts_hbm.1, f32[64,128]{1,0:T(8,128)} %a_in.1, f32[128,128]{1,0:T(8,128)} %b_in.1, f32[16,128]{1,0:T(8,128)} %c_in.1), custom_call_target="tpu_custom_call" | custom-call | tf_op jit(solution)/shard_map/pallas_call | solution.py:225
  51.2 1.4 %copy.10 = f32[64,128]{1,0:T(8,128)} copy(f32[64,128]{1,0:T(8,128)} %get-tuple-element.6) | data formatting | bytes 65536
  52.5 1.5 %copy.11 = f32[128,128]{1,0:T(8,128)} copy(f32[128,128]{1,0:T(8,128)} %get-tuple-element.7) | data formatting | bytes 131072
  54.0 1.3 %copy.12 = f32[16,128]{1,0:T(8,128)} copy(f32[16,128]{1,0:T(8,128)} %get-tuple-element.8) | data formatting | bytes 16384

commit v2 on v0

v2 whole, which is shorter than its diff:
```python
import functools
import math

import jax
import jax.numpy as jnp
from jax import lax
from jax.experimental import pallas as pl
from jax.experimental.pallas import tpu as pltpu
from jax.sharding import PartitionSpec as P

ITERS = 2
MESH = pl.DeviceIdType.MESH
F32 = jnp.float32
BF16 = jnp.bfloat16


def kernel(nr, nc, tile, rates, counts_hbm, a_in, b_in, c_in, a_out, b_out, c_out,
           counts, all_a, all_b, send_a, send_b, recv_a, recv_b, part_c, sum_c,
           held_a, trans_a, acc_a, acc_c, resid, scaled, mixed_t, grad_b,
           cnt_sem, ag_send, ag_recv, bg_send, bg_recv, ar_send, ar_recv, br_send, br_recv,
           c1_send, c1_recv, c2_send, c2_recv):
    row, col = lax.axis_index("rows"), lax.axis_index("cols")
    rate_a, rate_b, rate_c = rates
    own_a, rank = a_in.shape
    own_b = b_in.shape[0]
    depth = c_in.shape[0]
    tiles = counts.shape[1]
    per = tiles // nr
    width = tile // depth

    half = nc // 2
    near, spot = lax.div(col, half), lax.rem(col, half)
    near_peers = [near * half + lax.rem(spot + off, half) for off in range(1, half)]
    far_peers = [(1 - near) * half + lax.rem(spot + off, half) for off in range(half)]
    col_peers = near_peers + far_peers
    row_peers = [lax.rem(row + off, nr) for off in range(1, nr)]
    half_rows = half * own_a

    def load(h, t):
        return pltpu.make_async_copy(
            counts_hbm.at[pl.ds(pl.multiple_of(h * half_rows, half_rows), half_rows),
                          pl.ds(pl.multiple_of(t * tile, tile), tile)],
            counts.at[h, t], cnt_sem.at[h, t])

    def chunk(side, d):
        return lax.rem(row + side + d, nr)

    sides = (near, 1 - near)
    for side in range(2):
        for d in range(nr):
            for s in range(per):
                load(sides[side], chunk(side, d) * per + s).start()

    all_a[0, col] = a_in[...].astype(BF16)
    all_b[0, row] = b_in[...].astype(BF16)

    barrier = pltpu.get_barrier_semaphore()
    for p in col_peers:
        pl.semaphore_signal(barrier, inc=1, device_id={"cols": p}, device_id_type=MESH)
    for p in row_peers:
        pl.semaphore_signal(barrier, inc=1, device_id={"rows": p}, device_id_type=MESH)
    pl.semaphore_wait(barrier, nc + nr - 2)

    class Exchange:
        def __init__(self, send, recv, ss, rs, axis, me):
            self.args = (send, recv, ss, rs, axis, me)

        def to(self, p):
            send, recv, ss, rs, axis, me = self.args
            return pltpu.make_async_remote_copy(
                src_ref=recv.at[me] if send is None else send.at[p], dst_ref=recv.at[me],
                send_sem=ss.at[p], recv_sem=rs.at[me], device_id={axis: p}, device_id_type=MESH)

        def start(self, peers):
            for p in peers:
                self.to(p).start()

        def wait_recv(self, peers):
            send, recv, ss, rs, axis, me = self.args
            for p in peers:
                pltpu.make_async_remote_copy(
                    src_ref=recv.at[p], dst_ref=recv.at[p], send_sem=ss.at[p], recv_sem=rs.at[p],
                    device_id={axis: p}, device_id_type=MESH).wait_recv()

        def wait_send(self, peers):
            for p in peers:
                self.to(p).wait_send()

    pending = []
    local_a, local_b, shared_c = a_in[...], b_in[...], c_in[...]

    def gather(it):
        return (Exchange(None, all_a.at[it], ag_send.at[it], ag_recv.at[it], "cols", col),
                Exchange(None, all_b.at[it], bg_send.at[it], bg_recv.at[it], "rows", row))

    gather_a, gather_b = gather(0)
    gather_b.start(row_peers)
    gather_a.start(col_peers)

    for it in range(ITERS):
        pending += [(gather_a, col_peers), (gather_b, row_peers)]
        scatter_a = Exchange(send_a.at[it], recv_a.at[it], ar_send.at[it], ar_recv.at[it], "cols", col)
        scatter_b = Exchange(send_b.at[it], recv_b.at[it], br_send.at[it], br_recv.at[it], "rows", row)
        cols_c = Exchange(None, part_c.at[it], c1_send.at[it], c1_recv.at[it], "cols", col)
        rows_c = Exchange(None, sum_c.at[it], c2_send.at[it], c2_recv.at[it], "rows", row)
        pending += [(scatter_a, col_peers), (scatter_b, row_peers), (cols_c, col_peers), (rows_c, row_peers)]
        acc_a[...] = jnp.zeros_like(acc_a)
        acc_c[...] = jnp.zeros_like(acc_c)

        for side in range(2):
            h = sides[side]
            gather_a.wait_recv((near_peers, far_peers)[side])
            rows_a = all_a[it, pl.ds(h * half, half)].reshape(half_rows, rank)
            held_a[...] = rows_a
            trans_a[...] = rows_a.T

            def produce(q, s, slot):
                t = q * per + s
                if it == 0:
                    load(h, t).wait()
                if side == 0:
                    rows_b = all_b[it, q, pl.ds(s * width, width), :].astype(F32)
                    scaled[t] = (rows_b[:, None, :] * shared_c[None, :, :]).astype(BF16).reshape(tile, rank)
                log_rate = lax.dot_general(
                    held_a[...], scaled[t], (((1,), (1,)), ((), ())), preferred_element_type=F32)
                resid[slot] = (jnp.exp(log_rate) - counts[h, t].astype(F32)).astype(BF16)

            def consume(q, s, slot):
                t = q * per + s
                acc_a[h] += jnp.dot(resid[slot], scaled[t], preferred_element_type=F32)
                turned = jnp.dot(trans_a[...], resid[slot], preferred_element_type=F32)
                if side == 0:
                    mixed_t[t] = turned
                    return
                mixed = (mixed_t[t] + turned).T.reshape(width, depth, rank)
                rows_b = all_b[it, q, pl.ds(s * width, width), :].astype(F32)
                grad_b[pl.ds(s * width, width), :] = jnp.sum(mixed * shared_c[None, :, :], axis=1)
                acc_c[...] += jnp.sum(mixed * rows_b[:, None, :], axis=0)

            def step(d, carry):
                q = chunk(side, d)
                for s in range(per):
                    if s + 1 < per:
                        produce(q, s + 1, (s + 1) % 2)
                    else:
                        @pl.when(d < nr - 1)
                        def _():
                            q_next = chunk(side, d + 1)
                            if side == 0:
                                gather_b.wait_recv([q_next])
                            produce(q_next, 0, 0)
                    consume(q, s, s % 2)
                if side == 1:
                    send_b[it, q] = grad_b[...].astype(BF16)

                    @pl.when(d < nr - 1)
                    def _():
                        scatter_b.start([q])

                return carry

            produce(chunk(side, 0), 0, 0)
            lax.fori_loop(0, nr, step, 0)

            if side == 1:
                part_c[it, col] = acc_c[...].astype(BF16)
                cols_c.start(far_peers + near_peers)
            for k in range(half):
                send_a[it, h * half + k] = acc_a[h, pl.ds(k * own_a, own_a), :].astype(BF16)
            scatter_a.start((near_peers, far_peers)[side])

        last = it == ITERS - 1
        if not last:
            gather_a, gather_b = gather(it + 1)

        scatter_b.wait_recv(row_peers)
        recv_b[it, row] = jnp.zeros((own_b, rank), BF16)
        total_b = grad_b[...] + jnp.sum(recv_b[it].astype(F32), axis=0)
        local_b = local_b - rate_b * total_b
        if last:
            b_out[...] = local_b
        else:
            all_b[it + 1, row] = local_b.astype(BF16)
            gather_b.start(row_peers)

        cols_c.wait_recv(col_peers)
        sum_c[it, row] = jnp.sum(part_c[it].astype(F32), axis=0)
        rows_c.start(row_peers)

        scatter_a.wait_recv(col_peers)
        recv_a[it, col] = jnp.zeros((own_a, rank), BF16)
        total_a = acc_a[near, pl.ds(pl.multiple_of(spot * own_a, own_a), own_a), :] + jnp.sum(recv_a[it].astype(F32), axis=0)
        local_a = local_a - rate_a * total_a
        if last:
            a_out[...] = local_a
        else:
            all_a[it + 1, col] = local_a.astype(BF16)
            gather_a.start(col_peers)

        rows_c.wait_recv(row_peers)
        shared_c = shared_c - rate_c * jnp.sum(sum_c[it], axis=0)
        if last:
            c_out[...] = shared_c

    for group, peers in pending:
        group.wait_send(peers)


def finish(a, b, c, a_out, b_out, c_out):
    a_out[...] = a[...]
    b_out[...] = b[...]
    c_out[...] = c[...]


def local(nr, nc, counts, start_a, start_b, start_c):
    rows_here, flat_width = counts.shape
    own_a, rank = start_a.shape
    own_b = start_b.shape[0]
    depth = start_c.shape[0]
    cols_here = flat_width // depth
    total_i, total_j = rows_here * nr, cols_here * nc
    rates = (0.3 / math.sqrt(total_j * depth), 0.3 / math.sqrt(total_i * depth), 0.3 / math.sqrt(total_i * total_j))
    tile = 512
    tiles = flat_width // tile
    vmem = pl.BlockSpec(memory_space=pltpu.VMEM)
    dma = pltpu.SemaphoreType.DMA
    outs = [jax.ShapeDtypeStruct(x.shape, F32) for x in (start_a, start_b, start_c)]
    half_rows = rows_here // 2
    found = pl.pallas_call(
        functools.partial(kernel, nr, nc, tile, rates),
        out_shape=outs,
        in_specs=[pl.BlockSpec(memory_space=pl.ANY), vmem, vmem, vmem],
        out_specs=[vmem] * 3,
        scratch_shapes=[
            pltpu.VMEM((2, tiles, half_rows, tile), BF16),
            pltpu.VMEM((ITERS, nc, own_a, rank), BF16),
            pltpu.VMEM((ITERS, nr, own_b, rank), BF16),
            pltpu.VMEM((ITERS, nc, own_a, rank), BF16),
            pltpu.VMEM((ITERS, nr, own_b, rank), BF16),
            pltpu.VMEM((ITERS, nc, own_a, rank), BF16),
            pltpu.VMEM((ITERS, nr, own_b, rank), BF16),
            pltpu.VMEM((ITERS, nc, depth, rank), BF16),
            pltpu.VMEM((ITERS, nr, depth, rank), F32),
            pltpu.VMEM((half_rows, rank), BF16),
            pltpu.VMEM((rank, half_rows), BF16),
            pltpu.VMEM((2, half_rows, rank), F32),
            pltpu.VMEM((depth, rank), F32),
            pltpu.VMEM((2, half_rows, tile), BF16),
            pltpu.VMEM((tiles, tile, rank), BF16),
            pltpu.VMEM((tiles, rank, tile), F32),
            pltpu.VMEM((own_b, rank), F32),
            dma((2, tiles)),
            dma((ITERS, nc)), dma((ITERS, nc)), dma((ITERS, nr)), dma((ITERS, nr)),
            dma((ITERS, nc)), dma((ITERS, nc)), dma((ITERS, nr)), dma((ITERS, nr)),
            dma((ITERS, nc)), dma((ITERS, nc)), dma((ITERS, nr)), dma((ITERS, nr)),
        ],
        compiler_params=pltpu.CompilerParams(
            collective_id=0, has_side_effects=True, vmem_limit_bytes=56 * 1024 * 1024),
    )(counts, start_a, start_b, start_c)
    return pl.pallas_call(finish, out_shape=outs, in_specs=[vmem] * 3, out_specs=[vmem] * 3)(*found)


def solution(mesh):
    nr, nc = mesh.shape["rows"], mesh.shape["cols"]
    placed = (P("rows", "cols"), P(("rows", "cols"), None), P(("cols", "rows"), None), P())
    return jax.shard_map(
        functools.partial(local, nr, nc),
        mesh=mesh,
        in_specs=placed,
        out_specs=(P(("rows", "cols"), None), P(("cols", "rows"), None), P()),
        check_vma=False,
    )
```

time: 198 us -> 56 us (0.28)
  blocking collectives: 94 us -> 0 us
  Pallas kernels: 0 us -> 55.2 us
  matrix products: 33 us -> 0 us
  waiting for transfers between devices: 26 us -> 0 us
  local copies, waits for them, and re-layouts: 18.4 us -> 0 us
  between operations: 13.9 us -> 0.64 us
  other arithmetic: 11.4 us -> 0 us
    pallas_call x0 -> x2, Pallas kernels: none -> 55.2 us  [the longest x1 53.7 us: local(): pl.pallas_call(functools.partial(kernel, nr, nc, tile, rates), out_shape=...]
    psum x4 -> x0, blocking collectives: 47.2 us -> none  [the longest x2 29 us: local(): summed_c = lax.psum(partial_c, 'cols')]
    all_gather x4 -> x0, blocking collectives: 46.8 us -> none  [the longest x2 28.2 us: local(): lax.all_gather(local_a.astype(jnp.bfloat16), 'cols', axis=0, tiled=True)]
    dot_general x6 -> x0, matrix products: 33 us -> none  [the longest x2 16.8 us: local(): lax.dot_general(residual, low_a, (((0,), (0,)), ((), ())), preferred_elem...]
    reduce_scatter x4 -> x0, waiting for transfers between devices: 25.9 us -> none  [the longest x2 25.9 us: local(): summed_b = lax.psum_scatter(grad_b, 'rows', scatter_dimension=0, tiled=True)]
    unnamed x15 -> x0, local copies, waits for them, and re-layouts: 18.4 us -> none
    reduce_sum x2 -> x0, other arithmetic: 5.56 us -> none  [local(): grad_c = jnp.sum(mixed * low_b_wide[:, None, :], axis=0)]
    sub x4 -> x0, other arithmetic: 3.47 us -> none  [the longest x1 1.48 us: local(): local_b = local_b - rate_b * summed_b]
  transfers between devices with their start and end apart: 4 -> 0, of which waited for: 2 -> 0; matrix products, arithmetic and copies ran while one was open for 13% -> 0% of each run, Pallas kernels for 0% -> 0%
where the time goes in v2:
time: 56 us; the launch traced here: 55.8 us
  Pallas kernels  55.2 us (99%)
  between operations  0.64 us (1%)
    pallas_call x1, Pallas kernels, local(): pl.pallas_call(functools.partial(kernel, nr, nc, tile, rates), out_shape=...  53.7 us
    pallas_call x1, Pallas kernels, local(): pl.pallas_call(finish, out_shape=outs, in_specs=[vmem] * 3, out_specs=[vm...  1.48 us

profile of v2, /device:TPU:0, one launch (start us, length us, event | category | flops | bytes accessed | tf_op | source)
XLA Modules:
  0.0 55.8 jit_solution(6592618826728974410)
XLA Ops:
  0.6 53.7 %shard_map.67 = (f32[64,128]{1,0:T(8,128)}, f32[128,128]{1,0:T(8,128)}, f32[16,128]{1,0:T(8,128)}) custom-call(bf16[512,8192]{1,0:T(8,128)(2,1)} %counts_hbm.1, f32[64,128]{1,0:T(8,128)} %a_in.1, f32[128,128]{1,0:T(8,128)} %b_in.1, f32[16,128]{1,0:T(8,128)} %c_in.1), custom_call_target="tpu_custom_call" | custom-call | tf_op jit(solution)/shard_map/pallas_call | solution.py:229
  54.3 1.5 %shard_map.68 = (f32[64,128]{1,0:T(8,128)}, f32[128,128]{1,0:T(8,128)}, f32[16,128]{1,0:T(8,128)}) custom-call(f32[64,128]{1,0:T(8,128)} %get-tuple-element.6.a, f32[128,128]{1,0:T(8,128)} %get-tuple-element.7.b, f32[16,128]{1,0:T(8,128)} %get-tuple-element.8.c), custom_call_target="tpu_custom_call" | custom-call | tf_op jit(solution)/shard_map/pallas_call | solution.py:260

commit v3 on v2

--- a/solution.py
+++ b/solution.py
@@ -116,8 +116,6 @@
 
             def produce(q, s, slot):
                 t = q * per + s
-                if it == 0:
-                    load(h, t).wait()
                 if side == 0:
                     rows_b = all_b[it, q, pl.ds(s * width, width), :].astype(F32)
                     scaled[t] = (rows_b[:, None, :] * shared_c[None, :, :]).astype(BF16).reshape(tile, rank)
@@ -137,18 +135,26 @@
                 grad_b[pl.ds(s * width, width), :] = jnp.sum(mixed * shared_c[None, :, :], axis=1)
                 acc_c[...] += jnp.sum(mixed * rows_b[:, None, :], axis=0)
 
+            def ready(d):
+                q = chunk(side, d)
+                if it == 0:
+                    for s in range(per):
+                        load(h, q * per + s).wait()
+                return q
+
             def step(d, carry):
-                q = chunk(side, d)
+                q, q_next = chunk(side, d), chunk(side, d + 1)
+                if side == 0 or it == 0:
+                    @pl.when(d < nr - 1)
+                    def _():
+                        ready(d + 1)
+                        if side == 0:
+                            gather_b.wait_recv([q_next])
                 for s in range(per):
                     if s + 1 < per:
                         produce(q, s + 1, (s + 1) % 2)
                     else:
-                        @pl.when(d < nr - 1)
-                        def _():
-                            q_next = chunk(side, d + 1)
-                            if side == 0:
-                                gather_b.wait_recv([q_next])
-                            produce(q_next, 0, 0)
+                        produce(q_next, 0, 0)
                     consume(q, s, s % 2)
                 if side == 1:
                     send_b[it, q] = grad_b[...].astype(BF16)
@@ -159,7 +165,7 @@
 
                 return carry
 
-            produce(chunk(side, 0), 0, 0)
+            produce(ready(0), 0, 0)
             lax.fori_loop(0, nr, step, 0)
 
             if side == 1:

time: 56 us -> 47.3 us (0.84)
  Pallas kernels: 55.2 us -> 46.5 us
    pallas_call x1, Pallas kernels: 53.7 us -> 45 us  [local(): pl.pallas_call(functools.partial(kernel, nr, nc, tile, rates), out_shape=...]
where the time goes in v3:
time: 47.3 us; the launch traced here: 47.1 us
  Pallas kernels  46.5 us (98%)
  between operations  0.64 us (1%)
    pallas_call x1, Pallas kernels, local(): pl.pallas_call(functools.partial(kernel, nr, nc, tile, rates), out_shape=...  45 us
    pallas_call x1, Pallas kernels, local(): pl.pallas_call(finish, out_shape=outs, in_specs=[vmem] * 3, out_specs=[vm...  1.48 us

profile of v3, /device:TPU:0, one launch (start us, length us, event | category | flops | bytes accessed | tf_op | source)
XLA Modules:
  0.0 47.1 jit_solution(14708395882753198049)
XLA Ops:
  0.6 45.0 %shard_map.67 = (f32[64,128]{1,0:T(8,128)}, f32[128,128]{1,0:T(8,128)}, f32[16,128]{1,0:T(8,128)}) custom-call(bf16[512,8192]{1,0:T(8,128)(2,1)} %counts_hbm.1, f32[64,128]{1,0:T(8,128)} %a_in.1, f32[128,128]{1,0:T(8,128)} %b_in.1, f32[16,128]{1,0:T(8,128)} %c_in.1), custom_call_target="tpu_custom_call" | custom-call | tf_op jit(solution)/shard_map/pallas_call | solution.py:235
  45.6 1.5 %shard_map.68 = (f32[64,128]{1,0:T(8,128)}, f32[128,128]{1,0:T(8,128)}, f32[16,128]{1,0:T(8,128)}) custom-call(f32[64,128]{1,0:T(8,128)} %get-tuple-element.6.a, f32[128,128]{1,0:T(8,128)} %get-tuple-element.7.b, f32[16,128]{1,0:T(8,128)} %get-tuple-element.8.c), custom_call_target="tpu_custom_call" | custom-call | tf_op jit(solution)/shard_map/pallas_call | solution.py:266
